TPU v7x, 32 devices: a whole 2x2x4 slice. The times are simulated.
32 devices in a mesh: dp: 4 (over y, x), expert: 8 (over z, core).
Axes of the slice: x: 2, y: 2, z: 4, core: 2. Of those that a mesh axis runs over, the one named last changes fastest.
Arguments:
- tokens_in: bfloat16 [4096, 2048], P(('dp', 'expert')), may hold values from -6 to 6
- cotangent: bfloat16 [4096, 2048], P(('dp', 'expert')), may hold values from -6 to 6
- router_prob: float32 [4096], P(('dp', 'expert')), may hold values from 0.1 to 1
- expert_ids: int32 [4096, 1], P(('dp', 'expert')), may hold values from 0 to 3; in each aligned block of 128 rows (0 to 127, 128 to 255, ...) at most 40 rows name the same one
- w_gate: bfloat16 [8, 2048, 384], P('expert'), may hold values from -0.125 to 0.125
- w_up: bfloat16 [8, 2048, 384], P('expert'), may hold values from -0.125 to 0.125
- w_down: bfloat16 [8, 384, 2048], P('expert'), may hold values from -0.21875 to 0.21875
Outputs:
- layer_out: bfloat16 [4096, 2048], P(('dp', 'expert'))
- grad_input: bfloat16 [4096, 2048], P(('dp', 'expert'))
- grad_w_down: bfloat16 [8, 384, 2048], P('expert', 'dp')
Inputs may be any that keep to these rules, and one draw needn't show every extreme that they name: `expert_ids`: among the 128 tokens of one device no expert id appears more than 40 times.
All inputs are finite; a program needn't handle non-finite values.
Results may differ from a plain program's by a relative error of at most 0.012.
Values may be sent and summed in bfloat16 or wider, within the bound.
No kernel may reach another device: no remote copies, remote signals or barrier semaphores. Data moves between devices by JAX's collectives and lax.ppermute only.
A program may use at most 64 MiB of HBM per device.

v0:
```python
import functools

import jax
import jax.numpy as jnp
from jax import lax
from jax.experimental import pallas as pl
from jax.experimental.pallas import tpu as pltpu
from jax.sharding import PartitionSpec as P


NN = (((1,), (0,)), ((), ()))
NT = (((1,), (1,)), ((), ()))
TN = (((0,), (0,)), ((), ()))


def dot(a, b, dims=NN):
    return lax.dot_general(a, b, dims, preferred_element_type=jnp.float32)


def in_hbm(array):
    return pltpu.with_memory_space_constraint(array, pltpu.HBM)


def swap(block, axis, mask):
    route = [(i, i ^ mask) for i in range(lax.axis_size(axis))]
    return lax.ppermute(block, axis, route)


def slots_of(ids, chips, block):
    tok = ids.shape[1]
    chip = lax.axis_index("expert") // 2
    ranks = -(-chips // 8) * 8
    apart = jnp.bitwise_xor(ids, chip)
    match = lax.broadcasted_iota(jnp.int32, (ranks, tok), 0) == apart
    onehot = match.astype(jnp.float32)
    earlier = lax.broadcasted_iota(jnp.int32, (tok, tok), 0) < lax.broadcasted_iota(
        jnp.int32, (tok, tok), 1
    )
    before = dot(onehot.astype(jnp.bfloat16), earlier.astype(jnp.float32).astype(jnp.bfloat16))
    rank = jnp.sum(before * onehot, axis=0, keepdims=True).astype(jnp.int32)
    return apart * block + rank


def column_of(row):
    tok = row.shape[1]
    eye = lax.broadcasted_iota(jnp.int32, (tok, tok), 0) == lax.broadcasted_iota(
        jnp.int32, (tok, tok), 1
    )
    return jnp.sum(jnp.where(eye, row, 0.0), axis=1, keepdims=True)


def dispatch_body(chips, block, *refs):
    sources, out_refs, held, sems = refs[:4], refs[4 : 4 + chips], refs[4 + chips : -1], refs[-1]
    fetches = [pltpu.make_async_copy(sources[n], held[n], sems.at[n]) for n in range(4)]
    for fetch in fetches:
        fetch.start()
    ids_ref, prob_ref, x_ref, dy_ref = held
    fetch_x, fetch_dy = fetches[2:]
    fetches[0].wait()
    fetches[1].wait()
    tok = x_ref.shape[0]
    slot = slots_of(ids_ref[...], chips, block)
    rows = chips * block
    placing = (lax.broadcasted_iota(jnp.int32, (rows, tok), 0) == slot).astype(jnp.float32)
    placing = placing.astype(jnp.bfloat16)
    column = column_of(prob_ref[...])
    fetch_x.wait()
    send_x = dot(placing, x_ref[...]).astype(jnp.bfloat16)
    for j in range(chips):
        out_refs[j][:block, :] = send_x[j * block : (j + 1) * block]
    fetch_dy.wait()
    scaled = (column * dy_ref[...].astype(jnp.float32)).astype(jnp.bfloat16)
    send_dy = dot(placing, scaled).astype(jnp.bfloat16)
    for j in range(chips):
        out_refs[j][block:, :] = send_dy[j * block : (j + 1) * block]


def stage_body(*refs):
    count = len(refs) // 2
    sems = refs[-1]
    copies = [pltpu.make_async_copy(refs[n], refs[count + n], sems.at[n]) for n in range(count)]
    for copy in copies:
        copy.start()
    for copy in copies:
        copy.wait()


def stage(arrays):
    return pl.pallas_call(
        stage_body,
        in_specs=[pl.BlockSpec(memory_space=pltpu.HBM)] * len(arrays),
        out_specs=[pl.BlockSpec(memory_space=pltpu.VMEM)] * len(arrays),
        out_shape=[pltpu.VMEM(a.shape, a.dtype) for a in arrays],
        scratch_shapes=[pltpu.SemaphoreType.DMA((len(arrays),))],
        compiler_params=pltpu.CompilerParams(vmem_limit_bytes=8 << 20),
        cost_estimate=pl.CostEstimate(
            flops=0, bytes_accessed=sum(4 * a.size for a in arrays), transcendentals=0
        ),
        name="stage",
    )(*[in_hbm(a) for a in arrays])


def combine_body(chips, block, ids_ref, prob_ref, *refs):
    back, (out_ref, grad_ref) = refs[:chips], refs[chips:]
    tok = out_ref.shape[0]
    slot = slots_of(ids_ref[...], chips, block)
    rows = chips * block
    placing = (lax.broadcasted_iota(jnp.int32, (rows, tok), 0) == slot).astype(jnp.float32)
    placing = placing.astype(jnp.bfloat16)
    out = jnp.concatenate([ref[:block, :] for ref in back], axis=0)
    grad = jnp.concatenate([ref[block:, :] for ref in back], axis=0)
    out_ref[...] = (column_of(prob_ref[...]) * dot(placing, out, TN)).astype(jnp.bfloat16)
    grad_ref[...] = dot(placing, grad, TN).astype(jnp.bfloat16)


def expert_body(count, block, tile, *refs):
    chunks, refs = refs[:count], refs[count:]
    own, other, refs = refs[:3], refs[3:6], refs[6:]
    backs, (kept_ref, shared_ref, out, grad) = refs[:count], refs[count:]
    model = chunks[0].shape[1]
    units = kept_ref.shape[1]
    x = jnp.concatenate([ref[:block, :] for ref in chunks], axis=0)
    dy = jnp.concatenate([ref[block:, :] for ref in chunks], axis=0)
    shared_ref[:, :model] = dy
    for first in range(0, units, tile):
        part = slice(first, first + tile)
        gate_w, up_w = (
            jnp.concatenate([own[n][0, :, part], other[n][0, :, part]], axis=1) for n in (0, 1)
        )
        down_w = jnp.concatenate([own[2][0, part, :], other[2][0, part, :]], axis=0)
        gate = dot(x, gate_w)
        up = dot(x, up_w)
        grad_hidden = dot(dy, down_w, NT)
        sig = jax.nn.sigmoid(gate)
        active = gate * sig
        hidden = (active * up).astype(jnp.bfloat16)
        kept_ref[:, part] = hidden[:, :tile]
        shared_ref[:, model + first : model + first + tile] = hidden[:, tile:]
        grad_gate = (grad_hidden * up * sig * (1.0 + gate * (1.0 - sig))).astype(jnp.bfloat16)
        grad_up = (grad_hidden * active).astype(jnp.bfloat16)
        new_out = dot(hidden, down_w)
        new_grad = dot(grad_gate, gate_w, NT) + dot(grad_up, up_w, NT)
        if first:
            new_out, new_grad = out[...] + new_out, grad[...] + new_grad
        if first + tile < units:
            out[...], grad[...] = new_out, new_grad
            continue
        for n in range(count):
            backs[n][:block, :] = new_out[n * block : (n + 1) * block, :].astype(jnp.bfloat16)
            backs[n][block:, :] = new_grad[n * block : (n + 1) * block, :].astype(jnp.bfloat16)


def expert(chunks, own, other):
    count = len(chunks)
    block, model = chunks[0].shape[0] // 2, chunks[0].shape[1]
    units = own[0].shape[2]
    rows = count * block
    vmem = pl.BlockSpec(memory_space=pltpu.VMEM)
    results = pl.pallas_call(
        functools.partial(expert_body, count, block, 128),
        in_specs=[vmem] * (count + 6),
        out_specs=[vmem] * (count + 2),
        out_shape=[jax.ShapeDtypeStruct((2 * block, model), jnp.bfloat16)] * count
        + [
            jax.ShapeDtypeStruct((rows, units), jnp.bfloat16),
            jax.ShapeDtypeStruct((rows, model + units), jnp.bfloat16),
        ],
        scratch_shapes=[
            pltpu.VMEM((rows, model), jnp.float32),
            pltpu.VMEM((rows, model), jnp.float32),
        ],
        compiler_params=pltpu.CompilerParams(vmem_limit_bytes=28 << 20),
        cost_estimate=pl.CostEstimate(
            flops=24 * rows * model * units,
            bytes_accessed=12 * model * units + 8 * rows * model,
            transcendentals=2 * rows * units,
        ),
        name="expert",
    )(*chunks, *own, *other)
    return results[:count], results[count], results[count + 1]


def weight_body(chunk_count, groups, block, parts, *refs):
    chunks, kept = refs[:chunk_count], refs[chunk_count : chunk_count + groups]
    shared = refs[chunk_count + groups : chunk_count + 2 * groups]
    outs, term = refs[chunk_count + 2 * groups : -1], refs[-1]
    columns = term.shape[1]
    model = chunks[0].shape[1]
    here = pl.ds(pl.multiple_of(pl.program_id(0) * columns, columns), columns)
    hidden = jnp.concatenate(
        [ref[...] for ref in kept] + [ref[:, model:] for ref in shared], axis=0
    )
    dy = jnp.concatenate(
        [ref[block:, here] for ref in chunks] + [ref[:, here] for ref in shared], axis=0
    )
    term[...] = dot(hidden, dy, TN)
    if parts == 1:
        outs[0][...] = term[...].astype(jnp.bfloat16)
        return
    me = lax.axis_index("dp")
    height = term.shape[0] // parts
    for m in range(parts):
        first = pl.multiple_of(jnp.bitwise_xor(me, m) * height, 8)
        outs[m][...] = term[pl.ds(first, height), :].astype(jnp.bfloat16)


def weight_terms(chunks, kept, shared, parts):
    block, model = chunks[0].shape[0] // 2, chunks[0].shape[1]
    units = kept[0].shape[1]
    columns = 512
    full = lambda a: pl.BlockSpec(a.shape, lambda i: (0, 0))
    rows = 2 * sum(a.shape[0] for a in kept)
    return pl.pallas_call(
        functools.partial(weight_body, len(chunks), len(kept), block, parts),
        grid=(model // columns,),
        in_specs=[full(a) for a in (*chunks, *kept, *shared)],
        out_specs=[pl.BlockSpec((units // parts, columns), lambda i: (0, i))] * parts,
        out_shape=[jax.ShapeDtypeStruct((units // parts, model), jnp.bfloat16)] * parts,
        scratch_shapes=[pltpu.VMEM((units, columns), jnp.float32)],
        compiler_params=pltpu.CompilerParams(vmem_limit_bytes=16 << 20),
        cost_estimate=pl.CostEstimate(
            flops=2 * rows * model * units,
            bytes_accessed=2 * (rows * (model + units) + units * model),
            transcendentals=0,
        ),
        name="weight_terms",
    )(*chunks, *kept, *shared)


def plan(chips):
    each = max(1, chips // 4)
    groups = [list(range(g, g + each)) for g in range(0, chips, each)]
    if len(groups) > 1:
        groups = groups[:2:-1] + [groups[0] + groups[1]] + groups[2:3]
    return [j for group in groups for j in group if j], groups


def direct_sum(parts, units):
    return parts <= 8 and units % (8 * parts) == 0


def per_device(tokens_in, cotangent, router_prob, expert_ids, w_gate, w_up, w_down):
    chips = lax.axis_size("expert") // 2
    tok, model = tokens_in.shape
    most = 5 * tok // (4 * chips)
    block = -(-most // 8) * 8
    ids = expert_ids.reshape(1, tok)
    prob = router_prob.reshape(1, tok)
    sends = pl.pallas_call(
        functools.partial(dispatch_body, chips, block),
        in_specs=[pl.BlockSpec(memory_space=pltpu.HBM)] * 4,
        out_shape=[jax.ShapeDtypeStruct((2 * block, model), jnp.bfloat16)] * chips,
        scratch_shapes=[
            pltpu.VMEM((1, tok), jnp.int32),
            pltpu.VMEM((1, tok), jnp.float32),
            pltpu.VMEM((tok, model), jnp.bfloat16),
            pltpu.VMEM((tok, model), jnp.bfloat16),
            pltpu.SemaphoreType.DMA((4,)),
        ],
        compiler_params=pltpu.CompilerParams(vmem_limit_bytes=16 << 20),
        cost_estimate=pl.CostEstimate(
            flops=4 * chips * block * tok * model,
            bytes_accessed=4 * (chips * block + tok) * model,
            transcendentals=0,
        ),
        name="dispatch",
    )(*[in_hbm(a) for a in (ids, prob, tokens_in, cotangent)])
    own = (w_gate, w_up, w_down)
    order, groups = plan(chips)
    arrived = {0: sends[0]}
    for j in order:
        arrived[j] = swap(sends[j], "expert", 2 * j)
    other = tuple(swap(w, "expert", 1) for w in own)
    own = stage(own)
    kept, shared, backs = [], [], {}
    for group in groups:
        results, mine, theirs = expert([arrived[j] for j in group], own, other)
        for j, result in zip(group, results):
            backs[j] = swap(result, "expert", 2 * j) if j else result
        kept.append(mine)
        shared.append(swap(theirs, "expert", 1))
    parts = lax.axis_size("dp")
    direct = direct_sum(parts, w_down.shape[1])
    rows = [arrived[j] for group in groups for j in group]
    terms = weight_terms(rows, kept, shared, parts if direct else 1)
    if direct:
        total = terms[0].astype(jnp.float32)
        for m in range(1, parts):
            total = total + swap(terms[m], "dp", m).astype(jnp.float32)
        summed = total.astype(jnp.bfloat16)
    else:
        summed = lax.psum_scatter(terms[0], "dp", scatter_dimension=0, tiled=True)
    layer_out, grad_input = pl.pallas_call(
        functools.partial(combine_body, chips, block),
        out_shape=[jax.ShapeDtypeStruct((tok, model), jnp.bfloat16)] * 2,
        compiler_params=pltpu.CompilerParams(vmem_limit_bytes=16 << 20),
        cost_estimate=pl.CostEstimate(
            flops=4 * chips * block * tok * model,
            bytes_accessed=4 * (chips * block + tok) * model,
            transcendentals=0,
        ),
        name="combine",
    )(ids, prob, *[backs[j] for j in range(chips)])
    return layer_out, grad_input, summed[None]


def solution(mesh):
    placed = (
        P(("dp", "expert"), None),
        P(("dp", "expert"), None),
        P(("dp", "expert")),
        P(("dp", "expert"), None),
        P("expert", None, None),
        P("expert", None, None),
        P("expert", None, None),
    )

    return jax.shard_map(
        per_device,
        mesh=mesh,
        in_specs=placed,
        out_specs=(P(("dp", "expert"), None), P(("dp", "expert"), None), P("expert", "dp", None)),
        check_vma=False,
    )
```

profile of v0, /device:TPU:0, one launch (start us, length us, event | category | flops | bytes accessed | tf_op | source)
XLA Modules:
  0.0 76.0 jit_solution(4667987992288510899)
XLA Ops:
  0.6 0.6 collective-permute-start.1
  1.3 0.4 collective-permute-start.3
  1.7 1.8 %dispatch.1 = (bf16[80,2048]{1,0:T(8,128)(2,1)S(1)}, bf16[80,2048]{1,0:T(8,128)(2,1)S(1)}, bf16[80,2048]{1,0:T(8,128)(2,1)S(1)}, bf16[80,2048]{1,0:T(8,128)(2,1)S(1)}) custom-call(s32[1,128]{1,0:T(1,128)} %bitcast.4, f32[1,128]{1,0:T(1,128)} %bitcast.6, bf16[128,2048]{1,0:T(8,128)(2,1)} %refs_2_.2, bf16[128,2048]{1,0:T(8,128)(2,1)} %refs_3_.1), custom_call_target="tpu_custom_call" | custom-call | flops 167772160 | bytes 2359296 | tf_op jit(solution)/shard_map/dispatch/pallas_call | solution.py:249
  3.5 2.7 %collective-permute-start = (bf16[80,2048]{1,0:T(8,128)(2,1)S(1)}, bf16[80,2048]{1,0:T(8,128)(2,1)S(1)}, u32[]{:S(2)}, u32[]{:S(2)}) collective-permute-start(bf16[80,2048]{1,0:T(8,128)(2,1)S(1)} %get-tuple-element.27), channel_id=1, source_target_pairs={{0,2},{1,3},{2,0},{3,1},{4,6},{5,7},{6,4},{7,5},{8,10},{9,11},{10,... | collective-permute-start | bytes 983048 | tf_op jit(solution)/shard_map/ppermute | solution.py:26
  6.2 2.5 %collective-permute-start.7 = (bf16[80,2048]{1,0:T(8,128)(2,1)S(1)}, bf16[80,2048]{1,0:T(8,128)(2,1)S(1)}, u32[]{:S(2)}, u32[]{:S(2)}) collective-permute-start(bf16[80,2048]{1,0:T(8,128)(2,1)S(1)} %get-tuple-element.35), channel_id=1, source_target_pairs={{0,6},{1,7},{2,4},{3,5},{4,2},{5,3},{6,0},{7,1},{8,14},{9,15},{10,... | collective-permute-start | bytes 983048 | tf_op jit(solution)/shard_map/ppermute | solution.py:26
  8.6 5.8 %collective-permute-done.refs_1_.refs_2_ = bf16[80,2048]{1,0:T(8,128)(2,1)S(1)} collective-permute-done((bf16[80,2048]{1,0:T(8,128)(2,1)S(1)}, bf16[80,2048]{1,0:T(8,128)(2,1)S(1)}, u32[]{:S(2)}, u32[]{:S(2)}) %collective-permute-start) | collective-permute-done | bytes 327712 | tf_op jit(solution)/shard_map/ppermute | solution.py:26
  14.5 3.3 %collective-permute-start.5 = (bf16[80,2048]{1,0:T(8,128)(2,1)S(1)}, bf16[80,2048]{1,0:T(8,128)(2,1)S(1)}, u32[]{:S(2)}, u32[]{:S(2)}) collective-permute-start(bf16[80,2048]{1,0:T(8,128)(2,1)S(1)} %get-tuple-element.33), channel_id=1, source_target_pairs={{0,4},{1,5},{2,6},{3,7},{4,0},{5,1},{6,2},{7,3},{8,12},{9,13},{10,... | collective-permute-start | bytes 983048 | tf_op jit(solution)/shard_map/ppermute | solution.py:26
  17.8 2.4 %stage.1 = (bf16[1,2048,384]{2,1,0:T(8,128)(2,1)S(1)}, bf16[1,2048,384]{2,1,0:T(8,128)(2,1)S(1)}, bf16[1,384,2048]{2,1,0:T(8,128)(2,1)S(1)}) custom-call(bf16[1,2048,384]{2,1,0:T(8,128)(2,1)} %refs_0_.1, bf16[1,2048,384]{2,1,0:T(8,128)(2,1)} %refs_1_.1, bf16[1,384,2048]{2,1,0:T(8,128)(2,1)} %refs_2_.3), custom_call_target="tpu_custom_call" | custom-call | bytes 9437184 | tf_op jit(solution)/shard_map/stage/pallas_call | solution.py:89
  20.2 4.9 %expert.3 = (bf16[80,2048]{1,0:T(8,128)(2,1)S(1)}, bf16[80,2048]{1,0:T(8,128)(2,1)S(1)}, bf16[80,384]{1,0:T(8,128)(2,1)S(1)}, bf16[80,2432]{1,0:T(8,128)(2,1)S(1)}) custom-call(bf16[80,2048]{1,0:T(8,128)(2,1)S(1)} %get-tuple-element.26.refs_0_.refs_1_, bf16[80,2048]{1,0:T(8,128)(2,1)S(1)} %collective-permute-done.refs_1_.refs_2_, ...), custom_call_target="tpu_custom_call" | custom-call | flops 1509949440 | bytes 10747904 | tf_op jit(solution)/shard_map/expert/pallas_call | solution.py:159
  25.1 4.7 %expert.5 = (bf16[80,2048]{1,0:T(8,128)(2,1)S(1)}, bf16[40,384]{1,0:T(8,128)(2,1)S(1)}, bf16[40,2432]{1,0:T(8,128)(2,1)S(1)}) custom-call(bf16[80,2048]{1,0:T(8,128)(2,1)S(1)} %collective-permute-done.7.refs_0_, bf16[1,2048,384]{2,1,0:T(8,128)(2,1)S(1)} %get-tuple-element.28.refs_2_.refs_1_, bf16[1,2048,384]{2,1,0:T(8,128)(2,1)S(1)} %get-tuple-element.29.refs_3_.refs_2_, ...), custom_call_target="tpu_custom_call" | custom-call | flops 754974720 | bytes 10092544 | tf_op jit(solution)/shard_map/expert/pallas_call | solution.py:159
  29.9 0.6 collective-permute-start.9
  30.4 7.1 %collective-permute-start.8 = (bf16[80,2048]{1,0:T(8,128)(2,1)S(1)}, bf16[80,2048]{1,0:T(8,128)(2,1)S(1)}, u32[]{:S(2)}, u32[]{:S(2)}) collective-permute-start(bf16[80,2048]{1,0:T(8,128)(2,1)S(1)} %get-tuple-element.36), channel_id=1, source_target_pairs={{0,6},{1,7},{2,4},{3,5},{4,2},{5,3},{6,0},{7,1},{8,14},{9,15},{10,... | collective-permute-start | bytes 983048 | tf_op jit(solution)/shard_map/ppermute | solution.py:26
  37.9 4.7 %expert.4 = (bf16[80,2048]{1,0:T(8,128)(2,1)S(1)}, bf16[40,384]{1,0:T(8,128)(2,1)S(1)}, bf16[40,2432]{1,0:T(8,128)(2,1)S(1)}) custom-call(bf16[80,2048]{1,0:T(8,128)(2,1)S(1)} %collective-permute-done.5.refs_0_.refs_3_, bf16[1,2048,384]{2,1,0:T(8,128)(2,1)S(1)} %get-tuple-element.28.refs_2_.refs_1_, ...), custom_call_target="tpu_custom_call" | custom-call | flops 754974720 | bytes 10092544 | tf_op jit(solution)/shard_map/expert/pallas_call | solution.py:159
  42.8 1.3 %collective-permute-done.11.refs_9_ = bf16[40,2432]{1,0:T(8,128)(2,1)S(1)} collective-permute-done((bf16[40,2432]{1,0:T(8,128)(2,1)S(1)}, bf16[40,2432]{1,0:T(8,128)(2,1)S(1)}, u32[]{:S(2)}, u32[]{:S(2)}) %collective-permute-start.11) | collective-permute-done | bytes 194592 | tf_op jit(solution)/shard_map/ppermute | solution.py:26
  44.1 2.0 %weight_terms.1 = (bf16[96,2048]{1,0:T(8,128)(2,1)S(1)}, bf16[96,2048]{1,0:T(8,128)(2,1)S(1)}, bf16[96,2048]{1,0:T(8,128)(2,1)S(1)}, bf16[96,2048]{1,0:T(8,128)(2,1)S(1)}) custom-call(bf16[80,2048]{1,0:T(8,128)(2,1)S(1)} %collective-permute-done.7.refs_0_, bf16[80,2048]{1,0:T(8,128)(2,1)S(1)} %get-tuple-element.26.refs_0_.refs_1_, ...), custom_call_target="tpu_custom_call" | custom-call | flops 503316480 | bytes 3129344 | tf_op jit(solution)/shard_map/weight_terms/pallas_call | solution.py:213
  46.1 1.6 %collective-permute-start.12 = (bf16[96,2048]{1,0:T(8,128)(2,1)S(1)}, bf16[96,2048]{1,0:T(8,128)(2,1)S(1)}, u32[]{:S(2)}, u32[]{:S(2)}) collective-permute-start(bf16[96,2048]{1,0:T(8,128)(2,1)S(1)} %get-tuple-element.46), channel_id=1, source_target_pairs={{0,8},{8,0},{16,24},{24,16},{1,9},{9,1},{17,25},{25,17},{2,10},{10... | collective-permute-start | bytes 1179656 | tf_op jit(solution)/shard_map/ppermute | solution.py:26
  47.6 1.6 %collective-permute-start.13 = (bf16[96,2048]{1,0:T(8,128)(2,1)S(1)}, bf16[96,2048]{1,0:T(8,128)(2,1)S(1)}, u32[]{:S(2)}, u32[]{:S(2)}) collective-permute-start(bf16[96,2048]{1,0:T(8,128)(2,1)S(1)} %get-tuple-element.47), channel_id=1, source_target_pairs={{0,16},{8,24},{16,0},{24,8},{1,17},{9,25},{17,1},{25,9},{2,18},{10... | collective-permute-start | bytes 1179656 | tf_op jit(solution)/shard_map/ppermute | solution.py:26
  49.2 0.4 collective-permute-start.14
  49.6 1.7 %collective-permute-start.6 = (bf16[80,2048]{1,0:T(8,128)(2,1)S(1)}, bf16[80,2048]{1,0:T(8,128)(2,1)S(1)}, u32[]{:S(2)}, u32[]{:S(2)}) collective-permute-start(bf16[80,2048]{1,0:T(8,128)(2,1)S(1)} %get-tuple-element.34), channel_id=1, source_target_pairs={{0,4},{1,5},{2,6},{3,7},{4,0},{5,1},{6,2},{7,3},{8,12},{9,13},{10,... | collective-permute-start | bytes 983048 | tf_op jit(solution)/shard_map/ppermute | solution.py:26
  51.3 8.9 %collective-permute-start.4 = (bf16[80,2048]{1,0:T(8,128)(2,1)S(1)}, bf16[80,2048]{1,0:T(8,128)(2,1)S(1)}, u32[]{:S(2)}, u32[]{:S(2)}) collective-permute-start(bf16[80,2048]{1,0:T(8,128)(2,1)S(1)} %get-tuple-element.32), channel_id=1, source_target_pairs={{0,2},{1,3},{2,0},{3,1},{4,6},{5,7},{6,4},{7,5},{8,10},{9,11},{10,... | collective-permute-start | bytes 983048 | tf_op jit(solution)/shard_map/ppermute | solution.py:26
  60.3 6.4 %collective-permute-done.6.refs_2_ = bf16[80,2048]{1,0:T(8,128)(2,1)S(1)} collective-permute-done((bf16[80,2048]{1,0:T(8,128)(2,1)S(1)}, bf16[80,2048]{1,0:T(8,128)(2,1)S(1)}, u32[]{:S(2)}, u32[]{:S(2)}) %collective-permute-start.6) | collective-permute-done | bytes 327712 | tf_op jit(solution)/shard_map/ppermute | solution.py:26
  66.6 6.9 %collective-permute-done.4.refs_1_ = bf16[80,2048]{1,0:T(8,128)(2,1)S(1)} collective-permute-done((bf16[80,2048]{1,0:T(8,128)(2,1)S(1)}, bf16[80,2048]{1,0:T(8,128)(2,1)S(1)}, u32[]{:S(2)}, u32[]{:S(2)}) %collective-permute-start.4) | collective-permute-done | bytes 327712 | tf_op jit(solution)/shard_map/ppermute | solution.py:26
  73.6 1.4 %combine.1 = (bf16[128,2048]{1,0:T(8,128)(2,1)}, bf16[128,2048]{1,0:T(8,128)(2,1)}) custom-call(s32[1,128]{1,0:T(1,128)S(1)} %bitcast.5, f32[1,128]{1,0:T(1,128)S(1)} %bitcast.7, bf16[80,2048]{1,0:T(8,128)(2,1)S(1)} %get-tuple-element.31.refs_0_, bf16[80,2048]{1,0:T(8,128)(2,1)S(1)} %collective-permute-done.4.refs_1_, ...), custom_call_target="tpu_custom_call" | custom-call | flops 167772160 | bytes 2359296 | tf_op jit(solution)/shard_map/combine/pallas_call | solution.py:293
  75.0 1.0 %fusion = bf16[1,96,2048]{2,1,0:T(8,128)(2,1)} fusion(bf16[96,2048]{1,0:T(8,128)(2,1)S(1)} %collective-permute-done.14, bf16[96,2048]{1,0:T(8,128)(2,1)S(1)} %collective-permute-done.13, bf16[96,2048]{1,0:T(8,128)(2,1)S(1)} %collective-permute-done.12, bf16[96,2048]{1,0:T(8,128)(2,1)S(1)} %get-tuple-element.45), kind=kLoop, calls=%fused_computation.1 | loop fusion | flops 1572864 | bytes 1966080 | tf_op jit(solution)/shard_map/broadcast_in_dim | solution.py:304
  (18 shorter events, 0.7 us)
Async XLA Ops:
  0.6 19.5 %collective-permute-start.1 = (bf16[1,2048,384]{2,1,0:T(8,128)(2,1)}, bf16[1,2048,384]{2,1,0:T(8,128)(2,1)S(1)}, u32[]{:S(2)}, u32[]{:S(2)}) collective-permute-start(bf16[1,2048,384]{2,1,0:T(8,128)(2,1)} %refs_0_.1), channel_id=1, source_target_pairs={{0,1},{1,0},{2,3},{3,2},{4,5},{5,4},{6,7},{7,6},{8,9},{9,8},{10,11... | collective-permute-start | bytes 4718600 | tf_op jit(solution)/shard_map/ppermute | solution.py:26
  1.2 19.0 %collective-permute-start.2 = (bf16[1,2048,384]{2,1,0:T(8,128)(2,1)}, bf16[1,2048,384]{2,1,0:T(8,128)(2,1)S(1)}, u32[]{:S(2)}, u32[]{:S(2)}) collective-permute-start(bf16[1,2048,384]{2,1,0:T(8,128)(2,1)} %refs_1_.1), channel_id=1, source_target_pairs={{0,1},{1,0},{2,3},{3,2},{4,5},{5,4},{6,7},{7,6},{8,9},{9,8},{10,11... | collective-permute-start | bytes 4718600 | tf_op jit(solution)/shard_map/ppermute | solution.py:26
  1.3 18.9 %collective-permute-start.3 = (bf16[1,384,2048]{2,1,0:T(8,128)(2,1)}, bf16[1,384,2048]{2,1,0:T(8,128)(2,1)S(1)}, u32[]{:S(2)}, u32[]{:S(2)}) collective-permute-start(bf16[1,384,2048]{2,1,0:T(8,128)(2,1)} %refs_2_.3), channel_id=1, source_target_pairs={{0,1},{1,0},{2,3},{3,2},{4,5},{5,4},{6,7},{7,6},{8,9},{9,8},{10,11... | collective-permute-start | bytes 4718600 | tf_op jit(solution)/shard_map/ppermute | solution.py:26
  3.5 11.0 %collective-permute-start = (bf16[80,2048]{1,0:T(8,128)(2,1)S(1)}, bf16[80,2048]{1,0:T(8,128)(2,1)S(1)}, u32[]{:S(2)}, u32[]{:S(2)}) collective-permute-start(bf16[80,2048]{1,0:T(8,128)(2,1)S(1)} %get-tuple-element.27), channel_id=1, source_target_pairs={{0,2},{1,3},{2,0},{3,1},{4,6},{5,7},{6,4},{7,5},{8,10},{9,11},{10,... | collective-permute-start | bytes 983048 | tf_op jit(solution)/shard_map/ppermute | solution.py:26
  6.2 19.0 %collective-permute-start.7 = (bf16[80,2048]{1,0:T(8,128)(2,1)S(1)}, bf16[80,2048]{1,0:T(8,128)(2,1)S(1)}, u32[]{:S(2)}, u32[]{:S(2)}) collective-permute-start(bf16[80,2048]{1,0:T(8,128)(2,1)S(1)} %get-tuple-element.35), channel_id=1, source_target_pairs={{0,6},{1,7},{2,4},{3,5},{4,2},{5,3},{6,0},{7,1},{8,14},{9,15},{10,... | collective-permute-start | bytes 983048 | tf_op jit(solution)/shard_map/ppermute | solution.py:26
  14.5 23.4 %collective-permute-start.5 = (bf16[80,2048]{1,0:T(8,128)(2,1)S(1)}, bf16[80,2048]{1,0:T(8,128)(2,1)S(1)}, u32[]{:S(2)}, u32[]{:S(2)}) collective-permute-start(bf16[80,2048]{1,0:T(8,128)(2,1)S(1)} %get-tuple-element.33), channel_id=1, source_target_pairs={{0,4},{1,5},{2,6},{3,7},{4,0},{5,1},{6,2},{7,3},{8,12},{9,13},{10,... | collective-permute-start | bytes 983048 | tf_op jit(solution)/shard_map/ppermute | solution.py:26
  25.1 19.1 %collective-permute-start.10 = (bf16[80,2432]{1,0:T(8,128)(2,1)S(1)}, bf16[80,2432]{1,0:T(8,128)(2,1)S(1)}, u32[]{:S(2)}, u32[]{:S(2)}) collective-permute-start(bf16[80,2432]{1,0:T(8,128)(2,1)S(1)} %get-tuple-element.43), channel_id=1, source_target_pairs={{0,1},{1,0},{2,3},{3,2},{4,5},{5,4},{6,7},{7,6},{8,9},{9,8},{10,11... | collective-permute-start | bytes 1167368 | tf_op jit(solution)/shard_map/ppermute | solution.py:26
  29.9 12.9 %collective-permute-start.9 = (bf16[40,2432]{1,0:T(8,128)(2,1)S(1)}, bf16[40,2432]{1,0:T(8,128)(2,1)S(1)}, u32[]{:S(2)}, u32[]{:S(2)}) collective-permute-start(bf16[40,2432]{1,0:T(8,128)(2,1)S(1)} %get-tuple-element.42), channel_id=1, source_target_pairs={{0,1},{1,0},{2,3},{3,2},{4,5},{5,4},{6,7},{7,6},{8,9},{9,8},{10,11... | collective-permute-start | bytes 583688 | tf_op jit(solution)/shard_map/ppermute | solution.py:26
  30.4 20.9 %collective-permute-start.8 = (bf16[80,2048]{1,0:T(8,128)(2,1)S(1)}, bf16[80,2048]{1,0:T(8,128)(2,1)S(1)}, u32[]{:S(2)}, u32[]{:S(2)}) collective-permute-start(bf16[80,2048]{1,0:T(8,128)(2,1)S(1)} %get-tuple-element.36), channel_id=1, source_target_pairs={{0,6},{1,7},{2,4},{3,5},{4,2},{5,3},{6,0},{7,1},{8,14},{9,15},{10,... | collective-permute-start | bytes 983048 | tf_op jit(solution)/shard_map/ppermute | solution.py:26
  42.6 31.0 %copy-start = (s32[128,1]{0,1:T(1,128)S(1)}, s32[128,1]{0,1:T(1,128)}, u32[]{:S(2)}) copy-start(s32[128,1]{0,1:T(1,128)} %param.10) | copy-start | bytes 1540
  42.6 31.0 %copy-start.1 = (f32[128]{0:T(128)S(1)}, f32[128]{0:T(128)}, u32[]{:S(2)}) copy-start(f32[128]{0:T(128)} %param.9) | copy-start | bytes 1540
  42.6 1.5 %collective-permute-start.11 = (bf16[40,2432]{1,0:T(8,128)(2,1)S(1)}, bf16[40,2432]{1,0:T(8,128)(2,1)S(1)}, u32[]{:S(2)}, u32[]{:S(2)}) collective-permute-start(bf16[40,2432]{1,0:T(8,128)(2,1)S(1)} %get-tuple-element.44), channel_id=1, source_target_pairs={{0,1},{1,0},{2,3},{3,2},{4,5},{5,4},{6,7},{7,6},{8,9},{9,8},{10,11... | collective-permute-start | bytes 583688 | tf_op jit(solution)/shard_map/ppermute | solution.py:26
  46.1 28.9 %collective-permute-start.12 = (bf16[96,2048]{1,0:T(8,128)(2,1)S(1)}, bf16[96,2048]{1,0:T(8,128)(2,1)S(1)}, u32[]{:S(2)}, u32[]{:S(2)}) collective-permute-start(bf16[96,2048]{1,0:T(8,128)(2,1)S(1)} %get-tuple-element.46), channel_id=1, source_target_pairs={{0,8},{8,0},{16,24},{24,16},{1,9},{9,1},{17,25},{25,17},{2,10},{10... | collective-permute-start | bytes 1179656 | tf_op jit(solution)/shard_map/ppermute | solution.py:26
  47.6 27.4 %collective-permute-start.13 = (bf16[96,2048]{1,0:T(8,128)(2,1)S(1)}, bf16[96,2048]{1,0:T(8,128)(2,1)S(1)}, u32[]{:S(2)}, u32[]{:S(2)}) collective-permute-start(bf16[96,2048]{1,0:T(8,128)(2,1)S(1)} %get-tuple-element.47), channel_id=1, source_target_pairs={{0,16},{8,24},{16,0},{24,8},{1,17},{9,25},{17,1},{25,9},{2,18},{10... | collective-permute-start | bytes 1179656 | tf_op jit(solution)/shard_map/ppermute | solution.py:26
  49.2 25.8 %collective-permute-start.14 = (bf16[96,2048]{1,0:T(8,128)(2,1)S(1)}, bf16[96,2048]{1,0:T(8,128)(2,1)S(1)}, u32[]{:S(2)}, u32[]{:S(2)}) collective-permute-start(bf16[96,2048]{1,0:T(8,128)(2,1)S(1)} %get-tuple-element.48), channel_id=1, source_target_pairs={{0,24},{8,16},{16,8},{24,0},{1,25},{9,17},{17,9},{25,1},{2,26},{10... | collective-permute-start | bytes 1179656 | tf_op jit(solution)/shard_map/ppermute | solution.py:26
  49.6 17.0 %collective-permute-start.6 = (bf16[80,2048]{1,0:T(8,128)(2,1)S(1)}, bf16[80,2048]{1,0:T(8,128)(2,1)S(1)}, u32[]{:S(2)}, u32[]{:S(2)}) collective-permute-start(bf16[80,2048]{1,0:T(8,128)(2,1)S(1)} %get-tuple-element.34), channel_id=1, source_target_pairs={{0,4},{1,5},{2,6},{3,7},{4,0},{5,1},{6,2},{7,3},{8,12},{9,13},{10,... | collective-permute-start | bytes 983048 | tf_op jit(solution)/shard_map/ppermute | solution.py:26
  51.3 22.2 %collective-permute-start.4 = (bf16[80,2048]{1,0:T(8,128)(2,1)S(1)}, bf16[80,2048]{1,0:T(8,128)(2,1)S(1)}, u32[]{:S(2)}, u32[]{:S(2)}) collective-permute-start(bf16[80,2048]{1,0:T(8,128)(2,1)S(1)} %get-tuple-element.32), channel_id=1, source_target_pairs={{0,2},{1,3},{2,0},{3,1},{4,6},{5,7},{6,4},{7,5},{8,10},{9,11},{10,... | collective-permute-start | bytes 983048 | tf_op jit(solution)/shard_map/ppermute | solution.py:26
where the time goes:
time: 76.2 us; the launch traced here: 76 us
  starting transfers between devices  31.6 us (41%)
  Pallas kernels  21.8 us (29%)
  waiting for transfers between devices  20.8 us (27%)
  other arithmetic  0.98 us (1%)
    ppermute x15, starting transfers between devices, swap(): return lax.ppermute(block, axis, route)  31.6 us
    ppermute x15, waiting for transfers between devices, swap(): return lax.ppermute(block, axis, route)  20.8 us
    pallas_call x3, Pallas kernels, expert(): pl.pallas_call(functools.partial(expert_body, count, block, 128), in_spec...  14.3 us
    pallas_call x1, Pallas kernels, stage(): pl.pallas_call(stage_body, in_specs=[pl.BlockSpec(memory_space=pltpu.HBM)...  2.38 us
    pallas_call x1, Pallas kernels, weight_terms(): pl.pallas_call(functools.partial(weight_body, len(chunks), len(kept), blo...  1.96 us
    pallas_call x1, Pallas kernels, per_device(): pl.pallas_call(functools.partial(dispatch_body, chips, block), in_specs=[...  1.75 us
  transfers between devices with their start and end apart: 15, of which 5 were waited for; matrix products, arithmetic and copies ran while one was open for 0% of the time, Pallas kernels for 29%

commit v1 on v0

--- a/solution.py
+++ b/solution.py
@@ -113,29 +113,61 @@
     grad_ref[...] = dot(placing, grad, TN).astype(jnp.bfloat16)
 
 
-def expert_body(count, block, tile, *refs):
+def side_by_side(own, other, part):
+    wide = [jnp.concatenate([own[n][0, :, part], other[n][0, :, part]], axis=1) for n in (0, 1)]
+    if len(own) < 3:
+        return wide
+    return wide + [jnp.concatenate([own[2][0, part, :], other[2][0, part, :]], axis=0)]
+
+
+def forward_body(count, block, tile, *refs):
+    chunks, own, other = refs[:count], refs[count : count + 2], refs[count + 2 : count + 4]
+    kept_ref, shared_ref, gate_ref, up_ref = refs[count + 4 :]
+    model = chunks[0].shape[1]
+    x = jnp.concatenate([ref[:block, :] for ref in chunks], axis=0)
+    shared_ref[:, :model] = jnp.concatenate([ref[block:, :] for ref in chunks], axis=0)
+    for first in range(0, kept_ref.shape[1], tile):
+        part = slice(first, first + tile)
+        gate_w, up_w = side_by_side(own, other, part)
+        gate = dot(x, gate_w)
+        up = dot(x, up_w)
+        hidden = (gate * jax.nn.sigmoid(gate) * up).astype(jnp.bfloat16)
+        kept_ref[:, part] = hidden[:, :tile]
+        shared_ref[:, model + first : model + first + tile] = hidden[:, tile:]
+        gate_ref[:, 2 * first : 2 * (first + tile)] = gate
+        up_ref[:, 2 * first : 2 * (first + tile)] = up
+
+
+def expert_body(count, block, tile, ready, *refs):
     chunks, refs = refs[:count], refs[count:]
     own, other, refs = refs[:3], refs[3:6], refs[6:]
-    backs, (kept_ref, shared_ref, out, grad) = refs[:count], refs[count:]
+    if ready:
+        (kept_ref, shared_ref, gate_ref, up_ref), refs = refs[:4], refs[4:]
+        backs, (out, grad) = refs[:count], refs[count:]
+    else:
+        backs, (kept_ref, shared_ref, out, grad) = refs[:count], refs[count:]
     model = chunks[0].shape[1]
     units = kept_ref.shape[1]
-    x = jnp.concatenate([ref[:block, :] for ref in chunks], axis=0)
     dy = jnp.concatenate([ref[block:, :] for ref in chunks], axis=0)
-    shared_ref[:, :model] = dy
+    if not ready:
+        x = jnp.concatenate([ref[:block, :] for ref in chunks], axis=0)
+        shared_ref[:, :model] = dy
     for first in range(0, units, tile):
         part = slice(first, first + tile)
-        gate_w, up_w = (
-            jnp.concatenate([own[n][0, :, part], other[n][0, :, part]], axis=1) for n in (0, 1)
-        )
-        down_w = jnp.concatenate([own[2][0, part, :], other[2][0, part, :]], axis=0)
-        gate = dot(x, gate_w)
-        up = dot(x, up_w)
+        gate_w, up_w, down_w = side_by_side(own, other, part)
+        if ready:
+            gate = gate_ref[:, 2 * first : 2 * (first + tile)]
+            up = up_ref[:, 2 * first : 2 * (first + tile)]
+        else:
+            gate = dot(x, gate_w)
+            up = dot(x, up_w)
         grad_hidden = dot(dy, down_w, NT)
         sig = jax.nn.sigmoid(gate)
         active = gate * sig
         hidden = (active * up).astype(jnp.bfloat16)
-        kept_ref[:, part] = hidden[:, :tile]
-        shared_ref[:, model + first : model + first + tile] = hidden[:, tile:]
+        if not ready:
+            kept_ref[:, part] = hidden[:, :tile]
+            shared_ref[:, model + first : model + first + tile] = hidden[:, tile:]
         grad_gate = (grad_hidden * up * sig * (1.0 + gate * (1.0 - sig))).astype(jnp.bfloat16)
         grad_up = (grad_hidden * active).astype(jnp.bfloat16)
         new_out = dot(hidden, down_w)
@@ -150,34 +182,62 @@
             backs[n][block:, :] = new_grad[n * block : (n + 1) * block, :].astype(jnp.bfloat16)
 
 
-def expert(chunks, own, other):
+def forward(chunks, own, other):
     count = len(chunks)
     block, model = chunks[0].shape[0] // 2, chunks[0].shape[1]
     units = own[0].shape[2]
     rows = count * block
     vmem = pl.BlockSpec(memory_space=pltpu.VMEM)
-    results = pl.pallas_call(
-        functools.partial(expert_body, count, block, 128),
-        in_specs=[vmem] * (count + 6),
-        out_specs=[vmem] * (count + 2),
-        out_shape=[jax.ShapeDtypeStruct((2 * block, model), jnp.bfloat16)] * count
-        + [
+    return pl.pallas_call(
+        functools.partial(forward_body, count, block, 128),
+        in_specs=[vmem] * (count + 4),
+        out_specs=[vmem] * 4,
+        out_shape=[
             jax.ShapeDtypeStruct((rows, units), jnp.bfloat16),
             jax.ShapeDtypeStruct((rows, model + units), jnp.bfloat16),
+            jax.ShapeDtypeStruct((rows, 2 * units), jnp.float32),
+            jax.ShapeDtypeStruct((rows, 2 * units), jnp.float32),
         ],
+        compiler_params=pltpu.CompilerParams(vmem_limit_bytes=28 << 20),
+        cost_estimate=pl.CostEstimate(
+            flops=8 * rows * model * units,
+            bytes_accessed=8 * model * units + 4 * rows * model,
+            transcendentals=2 * rows * units,
+        ),
+        name="forward",
+    )(*chunks, *own[:2], *other[:2])
+
+
+def expert(chunks, own, other, ready=()):
+    count = len(chunks)
+    block, model = chunks[0].shape[0] // 2, chunks[0].shape[1]
+    units = own[0].shape[2]
+    rows = count * block
+    vmem = pl.BlockSpec(memory_space=pltpu.VMEM)
+    out_shape = [jax.ShapeDtypeStruct((2 * block, model), jnp.bfloat16)] * count
+    if not ready:
+        out_shape += [
+            jax.ShapeDtypeStruct((rows, units), jnp.bfloat16),
+            jax.ShapeDtypeStruct((rows, model + units), jnp.bfloat16),
+        ]
+    results = pl.pallas_call(
+        functools.partial(expert_body, count, block, 128, bool(ready)),
+        in_specs=[vmem] * (count + 6 + len(ready)),
+        out_specs=[vmem] * len(out_shape),
+        out_shape=out_shape,
         scratch_shapes=[
             pltpu.VMEM((rows, model), jnp.float32),
             pltpu.VMEM((rows, model), jnp.float32),
         ],
         compiler_params=pltpu.CompilerParams(vmem_limit_bytes=28 << 20),
         cost_estimate=pl.CostEstimate(
-            flops=24 * rows * model * units,
+            flops=(16 if ready else 24) * rows * model * units,
             bytes_accessed=12 * model * units + 8 * rows * model,
             transcendentals=2 * rows * units,
         ),
         name="expert",
-    )(*chunks, *own, *other)
-    return results[:count], results[count], results[count + 1]
+    )(*chunks, *own, *other, *ready)
+    return results[:count], results[count:]
 
 
 def weight_body(chunk_count, groups, block, parts, *refs):
@@ -225,6 +285,27 @@
         ),
         name="weight_terms",
     )(*chunks, *kept, *shared)
+
+
+def add_body(*refs):
+    total = refs[0][...].astype(jnp.float32)
+    for ref in refs[1:-1]:
+        total = total + ref[...].astype(jnp.float32)
+    refs[-1][...] = total.astype(jnp.bfloat16)
+
+
+def add_terms(terms):
+    return pl.pallas_call(
+        add_body,
+        out_shape=jax.ShapeDtypeStruct(terms[0].shape, jnp.bfloat16),
+        compiler_params=pltpu.CompilerParams(vmem_limit_bytes=8 << 20),
+        cost_estimate=pl.CostEstimate(
+            flops=len(terms) * terms[0].size,
+            bytes_accessed=2 * (len(terms) + 1) * terms[0].size,
+            transcendentals=0,
+        ),
+        name="add_terms",
+    )(*terms)
 
 
 def plan(chips):
@@ -273,21 +354,26 @@
     other = tuple(swap(w, "expert", 1) for w in own)
     own = stage(own)
     kept, shared, backs = [], [], {}
-    for group in groups:
-        results, mine, theirs = expert([arrived[j] for j in group], own, other)
-        for j, result in zip(group, results):
-            backs[j] = swap(result, "expert", 2 * j) if j else result
-        kept.append(mine)
-        shared.append(swap(theirs, "expert", 1))
+    for g, group in enumerate(groups):
+        chunks = [arrived[j] for j in group]
+        if g == len(groups) - 1:
+            saved = forward(chunks, own, other)
+        else:
+            results, saved = expert(chunks, own, other)
+            for j, result in zip(group, results):
+                backs[j] = swap(result, "expert", 2 * j) if j else result
+        kept.append(saved[0])
+        shared.append(swap(saved[1], "expert", 1))
+    results, _ = expert(chunks, own, other, saved)
+    for j, result in zip(groups[-1], results):
+        backs[j] = swap(result, "expert", 2 * j) if j else result
     parts = lax.axis_size("dp")
     direct = direct_sum(parts, w_down.shape[1])
     rows = [arrived[j] for group in groups for j in group]
     terms = weight_terms(rows, kept, shared, parts if direct else 1)
     if direct:
-        total = terms[0].astype(jnp.float32)
-        for m in range(1, parts):
-            total = total + swap(terms[m], "dp", m).astype(jnp.float32)
-        summed = total.astype(jnp.bfloat16)
+        spread = [swap(terms[m], "dp", m) for m in range(1, parts)]
+        summed = add_terms([terms[0], *spread])
     else:
         summed = lax.psum_scatter(terms[0], "dp", scatter_dimension=0, tiled=True)
     layer_out, grad_input = pl.pallas_call(

time: 76.2 us -> 72.6 us (0.953)
  starting transfers between devices: 31.6 us -> 14.5 us
  waiting for transfers between devices: 20.8 us -> 33.8 us
  Pallas kernels: 21.8 us -> 23.3 us
  other arithmetic: 0.98 us -> 0 us
    ppermute x15, starting transfers between devices: 31.6 us -> 14.5 us  [swap(): return lax.ppermute(block, axis, route)]
    ppermute x15, waiting for transfers between devices: 20.8 us -> 33.8 us  [swap(): return lax.ppermute(block, axis, route)]
    pallas_call x3 -> x5, Pallas kernels: 14.3 us -> 15.8 us  [the longest x3 13.6 us: expert(): pl.pallas_call(functools.partial(expert_body, count, block, 128, bool(rea...]
    broadcast_in_dim x1 -> x0, other arithmetic: 0.98 us -> none  [per_device(): return (layer_out, grad_input, summed[None])]
  transfers between devices with their start and end apart: 15 -> 15, of which waited for: 5 -> 4; matrix products, arithmetic and copies ran while one was open for 0% -> 0% of each run, Pallas kernels for 29% -> 31%
where the time goes in v1:
time: 72.6 us; the launch traced here: 72.4 us
  waiting for transfers between devices  33.8 us (47%)
  Pallas kernels  23.3 us (32%)
  starting transfers between devices  14.5 us (20%)
  between operations  0.78 us (1%)
    ppermute x15, waiting for transfers between devices, swap(): return lax.ppermute(block, axis, route)  33.8 us
    ppermute x15, starting transfers between devices, swap(): return lax.ppermute(block, axis, route)  14.5 us
    pallas_call x3, Pallas kernels, expert(): pl.pallas_call(functools.partial(expert_body, count, block, 128, bool(rea...  13.6 us
    pallas_call x1, Pallas kernels, stage(): pl.pallas_call(stage_body, in_specs=[pl.BlockSpec(memory_space=pltpu.HBM)...  2.38 us
    pallas_call x1, Pallas kernels, weight_terms(): pl.pallas_call(functools.partial(weight_body, len(chunks), len(kept), blo...  1.95 us
    pallas_call x1, Pallas kernels, per_device(): pl.pallas_call(functools.partial(dispatch_body, chips, block), in_specs=[...  1.75 us
  transfers between devices with their start and end apart: 15, of which 4 were waited for; matrix products, arithmetic and copies ran while one was open for 0% of the time, Pallas kernels for 31%

profile of v1, /device:TPU:0, one launch (start us, length us, event | category | flops | bytes accessed | tf_op | source)
XLA Modules:
  0.0 72.4 jit_solution(15710215619382850278)
XLA Ops:
  0.6 0.6 collective-permute-start.1
  1.3 0.4 collective-permute-start.3
  1.7 1.8 %dispatch.1 = (bf16[80,2048]{1,0:T(8,128)(2,1)S(1)}, bf16[80,2048]{1,0:T(8,128)(2,1)S(1)}, bf16[80,2048]{1,0:T(8,128)(2,1)S(1)}, bf16[80,2048]{1,0:T(8,128)(2,1)S(1)}) custom-call(s32[1,128]{1,0:T(1,128)} %bitcast.3, f32[1,128]{1,0:T(1,128)} %bitcast.5, bf16[128,2048]{1,0:T(8,128)(2,1)} %refs_2_.2, bf16[128,2048]{1,0:T(8,128)(2,1)} %refs_3_.1), custom_call_target="tpu_custom_call" | custom-call | flops 167772160 | bytes 2359296 | tf_op jit(solution)/shard_map/dispatch/pallas_call | solution.py:330
  3.5 2.7 %collective-permute-start = (bf16[80,2048]{1,0:T(8,128)(2,1)S(1)}, bf16[80,2048]{1,0:T(8,128)(2,1)S(1)}, u32[]{:S(2)}, u32[]{:S(2)}) collective-permute-start(bf16[80,2048]{1,0:T(8,128)(2,1)S(1)} %get-tuple-element.28), channel_id=1, source_target_pairs={{0,2},{1,3},{2,0},{3,1},{4,6},{5,7},{6,4},{7,5},{8,10},{9,11},{10,... | collective-permute-start | bytes 983048 | tf_op jit(solution)/shard_map/ppermute | solution.py:26
  6.2 2.6 %collective-permute-start.5 = (bf16[80,2048]{1,0:T(8,128)(2,1)S(1)}, bf16[80,2048]{1,0:T(8,128)(2,1)S(1)}, u32[]{:S(2)}, u32[]{:S(2)}) collective-permute-start(bf16[80,2048]{1,0:T(8,128)(2,1)S(1)} %get-tuple-element.34), channel_id=1, source_target_pairs={{0,4},{1,5},{2,6},{3,7},{4,0},{5,1},{6,2},{7,3},{8,12},{9,13},{10,... | collective-permute-start | bytes 983048 | tf_op jit(solution)/shard_map/ppermute | solution.py:26
  8.8 12.6 %collective-permute-done.refs_1_.refs_2_ = bf16[80,2048]{1,0:T(8,128)(2,1)S(1)} collective-permute-done((bf16[80,2048]{1,0:T(8,128)(2,1)S(1)}, bf16[80,2048]{1,0:T(8,128)(2,1)S(1)}, u32[]{:S(2)}, u32[]{:S(2)}) %collective-permute-start) | collective-permute-done | bytes 327712 | tf_op jit(solution)/shard_map/ppermute | solution.py:26
  21.4 2.6 %collective-permute-start.7 = (bf16[80,2048]{1,0:T(8,128)(2,1)S(1)}, bf16[80,2048]{1,0:T(8,128)(2,1)S(1)}, u32[]{:S(2)}, u32[]{:S(2)}) collective-permute-start(bf16[80,2048]{1,0:T(8,128)(2,1)S(1)} %get-tuple-element.39), channel_id=1, source_target_pairs={{0,6},{1,7},{2,4},{3,5},{4,2},{5,3},{6,0},{7,1},{8,14},{9,15},{10,... | collective-permute-start | bytes 983048 | tf_op jit(solution)/shard_map/ppermute | solution.py:26
  24.0 2.4 %stage.1 = (bf16[1,2048,384]{2,1,0:T(8,128)(2,1)S(1)}, bf16[1,2048,384]{2,1,0:T(8,128)(2,1)S(1)}, bf16[1,384,2048]{2,1,0:T(8,128)(2,1)S(1)}) custom-call(bf16[1,2048,384]{2,1,0:T(8,128)(2,1)} %refs_0_.1, bf16[1,2048,384]{2,1,0:T(8,128)(2,1)} %refs_1_.1, bf16[1,384,2048]{2,1,0:T(8,128)(2,1)} %refs_2_.3), custom_call_target="tpu_custom_call" | custom-call | bytes 9437184 | tf_op jit(solution)/shard_map/stage/pallas_call | solution.py:89
  26.4 4.8 %expert.3 = (bf16[80,2048]{1,0:T(8,128)(2,1)S(1)}, bf16[80,2048]{1,0:T(8,128)(2,1)S(1)}, bf16[80,384]{1,0:T(8,128)(2,1)S(1)}, bf16[80,2432]{1,0:T(8,128)(2,1)S(1)}) custom-call(bf16[80,2048]{1,0:T(8,128)(2,1)S(1)} %get-tuple-element.27.refs_0_.refs_1_, bf16[80,2048]{1,0:T(8,128)(2,1)S(1)} %collective-permute-done.refs_1_.refs_2_, ...), custom_call_target="tpu_custom_call" | custom-call | flops 1509949440 | bytes 10747904 | tf_op jit(solution)/shard_map/expert/pallas_call | solution.py:223
  31.4 1.2 %forward.1 = (bf16[40,384]{1,0:T(8,128)(2,1)S(1)}, bf16[40,2432]{1,0:T(8,128)(2,1)S(1)}, f32[40,768]{1,0:T(8,128)S(1)}, f32[40,768]{1,0:T(8,128)S(1)}) custom-call(bf16[80,2048]{1,0:T(8,128)(2,1)S(1)} %collective-permute-done.5.refs_0_.refs_3_, bf16[1,2048,384]{2,1,0:T(8,128)(2,1)S(1)} %get-tuple-element.29.refs_2_.refs_1_, ...), custom_call_target="tpu_custom_call" | custom-call | flops 251658240 | bytes 6619136 | tf_op jit(solution)/shard_map/forward/pallas_call | solution.py:191
  32.6 0.6 collective-permute-start.11
  33.1 4.1 %expert.4 = bf16[80,2048]{1,0:T(8,128)(2,1)S(1)} custom-call(bf16[80,2048]{1,0:T(8,128)(2,1)S(1)} %collective-permute-done.5.refs_0_.refs_3_, bf16[1,2048,384]{2,1,0:T(8,128)(2,1)S(1)} %get-tuple-element.29.refs_2_.refs_1_, bf16[1,2048,384]{2,1,0:T(8,128)(2,1)S(1)} %get-tuple-element.30.refs_3_.refs_2_, ...), custom_call_target="tpu_custom_call" | custom-call | flops 503316480 | bytes 10092544 | tf_op jit(solution)/shard_map/expert/pallas_call | solution.py:223
  37.3 4.7 %expert.5 = (bf16[80,2048]{1,0:T(8,128)(2,1)S(1)}, bf16[40,384]{1,0:T(8,128)(2,1)S(1)}, bf16[40,2432]{1,0:T(8,128)(2,1)S(1)}) custom-call(bf16[80,2048]{1,0:T(8,128)(2,1)S(1)} %collective-permute-done.7.refs_0_, bf16[1,2048,384]{2,1,0:T(8,128)(2,1)S(1)} %get-tuple-element.29.refs_2_.refs_1_, bf16[1,2048,384]{2,1,0:T(8,128)(2,1)S(1)} %get-tuple-element.30.refs_3_.refs_2_, ...), custom_call_target="tpu_custom_call" | custom-call | flops 754974720 | bytes 10092544 | tf_op jit(solution)/shard_map/expert/pallas_call | solution.py:223
  42.1 0.1 collective-permute-start.9
  42.2 1.4 %collective-permute-done.9.refs_7_ = bf16[40,2432]{1,0:T(8,128)(2,1)S(1)} collective-permute-done((bf16[40,2432]{1,0:T(8,128)(2,1)S(1)}, bf16[40,2432]{1,0:T(8,128)(2,1)S(1)}, u32[]{:S(2)}, u32[]{:S(2)}) %collective-permute-start.9) | collective-permute-done | bytes 194592 | tf_op jit(solution)/shard_map/ppermute | solution.py:26
  43.6 2.0 %weight_terms.1 = (bf16[96,2048]{1,0:T(8,128)(2,1)S(1)}, bf16[96,2048]{1,0:T(8,128)(2,1)S(1)}, bf16[96,2048]{1,0:T(8,128)(2,1)S(1)}, bf16[96,2048]{1,0:T(8,128)(2,1)S(1)}) custom-call(bf16[80,2048]{1,0:T(8,128)(2,1)S(1)} %collective-permute-done.7.refs_0_, bf16[80,2048]{1,0:T(8,128)(2,1)S(1)} %get-tuple-element.27.refs_0_.refs_1_, ...), custom_call_target="tpu_custom_call" | custom-call | flops 503316480 | bytes 3129344 | tf_op jit(solution)/shard_map/weight_terms/pallas_call | solution.py:273
  45.5 1.6 %collective-permute-start.12 = (bf16[96,2048]{1,0:T(8,128)(2,1)S(1)}, bf16[96,2048]{1,0:T(8,128)(2,1)S(1)}, u32[]{:S(2)}, u32[]{:S(2)}) collective-permute-start(bf16[96,2048]{1,0:T(8,128)(2,1)S(1)} %get-tuple-element.48), channel_id=1, source_target_pairs={{0,8},{8,0},{16,24},{24,16},{1,9},{9,1},{17,25},{25,17},{2,10},{10... | collective-permute-start | bytes 1179656 | tf_op jit(solution)/shard_map/ppermute | solution.py:26
  47.1 1.6 %collective-permute-start.13 = (bf16[96,2048]{1,0:T(8,128)(2,1)S(1)}, bf16[96,2048]{1,0:T(8,128)(2,1)S(1)}, u32[]{:S(2)}, u32[]{:S(2)}) collective-permute-start(bf16[96,2048]{1,0:T(8,128)(2,1)S(1)} %get-tuple-element.49), channel_id=1, source_target_pairs={{0,16},{8,24},{16,0},{24,8},{1,17},{9,25},{17,1},{25,9},{2,18},{10... | collective-permute-start | bytes 1179656 | tf_op jit(solution)/shard_map/ppermute | solution.py:26
  48.7 0.4 collective-permute-start.14
  49.1 1.2 %collective-permute-start.8 = (bf16[80,2048]{1,0:T(8,128)(2,1)S(1)}, bf16[80,2048]{1,0:T(8,128)(2,1)S(1)}, u32[]{:S(2)}, u32[]{:S(2)}) collective-permute-start(bf16[80,2048]{1,0:T(8,128)(2,1)S(1)} %get-tuple-element.40), channel_id=1, source_target_pairs={{0,6},{1,7},{2,4},{3,5},{4,2},{5,3},{6,0},{7,1},{8,14},{9,15},{10,... | collective-permute-start | bytes 983048 | tf_op jit(solution)/shard_map/ppermute | solution.py:26
  50.3 10.2 %collective-permute-done.6.refs_2_ = bf16[80,2048]{1,0:T(8,128)(2,1)S(1)} collective-permute-done((bf16[80,2048]{1,0:T(8,128)(2,1)S(1)}, bf16[80,2048]{1,0:T(8,128)(2,1)S(1)}, u32[]{:S(2)}, u32[]{:S(2)}) %collective-permute-start.6) | collective-permute-done | bytes 327712 | tf_op jit(solution)/shard_map/ppermute | solution.py:26
  60.5 9.5 %collective-permute-done.4.refs_1_ = bf16[80,2048]{1,0:T(8,128)(2,1)S(1)} collective-permute-done((bf16[80,2048]{1,0:T(8,128)(2,1)S(1)}, bf16[80,2048]{1,0:T(8,128)(2,1)S(1)}, u32[]{:S(2)}, u32[]{:S(2)}) %collective-permute-start.4) | collective-permute-done | bytes 327712 | tf_op jit(solution)/shard_map/ppermute | solution.py:26
  70.1 1.4 %combine.1 = (bf16[128,2048]{1,0:T(8,128)(2,1)}, bf16[128,2048]{1,0:T(8,128)(2,1)}) custom-call(s32[1,128]{1,0:T(1,128)S(1)} %bitcast.4, f32[1,128]{1,0:T(1,128)S(1)} %bitcast.6, bf16[80,2048]{1,0:T(8,128)(2,1)S(1)} %get-tuple-element.32.refs_0_, bf16[80,2048]{1,0:T(8,128)(2,1)S(1)} %collective-permute-done.4.refs_1_, ...), custom_call_target="tpu_custom_call" | custom-call | flops 167772160 | bytes 2359296 | tf_op jit(solution)/shard_map/combine/pallas_call | solution.py:379
  71.5 0.9 %add_terms.1 = bf16[96,2048]{1,0:T(8,128)(2,1)} custom-call(bf16[96,2048]{1,0:T(8,128)(2,1)S(1)} %get-tuple-element.47.refs_0_, bf16[96,2048]{1,0:T(8,128)(2,1)S(1)} %collective-permute-done.12.refs_1_, bf16[96,2048]{1,0:T(8,128)(2,1)S(1)} %collective-permute-done.13.refs_2_, bf16[96,2048]{1,0:T(8,128)(2,1)S(1)} %collective-permute-done.14.refs_3_), custom_call_target="tpu_custom_call" | custom-call | flops 786432 | bytes 1966080 | tf_op jit(solution)/shard_map/add_terms/pallas_call | solution.py:298
  (19 shorter events, 0.3 us)
Async XLA Ops:
  0.6 25.8 %collective-permute-start.1 = (bf16[1,2048,384]{2,1,0:T(8,128)(2,1)}, bf16[1,2048,384]{2,1,0:T(8,128)(2,1)S(1)}, u32[]{:S(2)}, u32[]{:S(2)}) collective-permute-start(bf16[1,2048,384]{2,1,0:T(8,128)(2,1)} %refs_0_.1), channel_id=1, source_target_pairs={{0,1},{1,0},{2,3},{3,2},{4,5},{5,4},{6,7},{7,6},{8,9},{9,8},{10,11... | collective-permute-start | bytes 4718600 | tf_op jit(solution)/shard_map/ppermute | solution.py:26
  1.2 25.2 %collective-permute-start.2 = (bf16[1,2048,384]{2,1,0:T(8,128)(2,1)}, bf16[1,2048,384]{2,1,0:T(8,128)(2,1)S(1)}, u32[]{:S(2)}, u32[]{:S(2)}) collective-permute-start(bf16[1,2048,384]{2,1,0:T(8,128)(2,1)} %refs_1_.1), channel_id=1, source_target_pairs={{0,1},{1,0},{2,3},{3,2},{4,5},{5,4},{6,7},{7,6},{8,9},{9,8},{10,11... | collective-permute-start | bytes 4718600 | tf_op jit(solution)/shard_map/ppermute | solution.py:26
  1.3 25.2 %collective-permute-start.3 = (bf16[1,384,2048]{2,1,0:T(8,128)(2,1)}, bf16[1,384,2048]{2,1,0:T(8,128)(2,1)S(1)}, u32[]{:S(2)}, u32[]{:S(2)}) collective-permute-start(bf16[1,384,2048]{2,1,0:T(8,128)(2,1)} %refs_2_.3), channel_id=1, source_target_pairs={{0,1},{1,0},{2,3},{3,2},{4,5},{5,4},{6,7},{7,6},{8,9},{9,8},{10,11... | collective-permute-start | bytes 4718600 | tf_op jit(solution)/shard_map/ppermute | solution.py:26
  3.5 17.9 %collective-permute-start = (bf16[80,2048]{1,0:T(8,128)(2,1)S(1)}, bf16[80,2048]{1,0:T(8,128)(2,1)S(1)}, u32[]{:S(2)}, u32[]{:S(2)}) collective-permute-start(bf16[80,2048]{1,0:T(8,128)(2,1)S(1)} %get-tuple-element.28), channel_id=1, source_target_pairs={{0,2},{1,3},{2,0},{3,1},{4,6},{5,7},{6,4},{7,5},{8,10},{9,11},{10,... | collective-permute-start | bytes 983048 | tf_op jit(solution)/shard_map/ppermute | solution.py:26
  6.2 25.2 %collective-permute-start.5 = (bf16[80,2048]{1,0:T(8,128)(2,1)S(1)}, bf16[80,2048]{1,0:T(8,128)(2,1)S(1)}, u32[]{:S(2)}, u32[]{:S(2)}) collective-permute-start(bf16[80,2048]{1,0:T(8,128)(2,1)S(1)} %get-tuple-element.34), channel_id=1, source_target_pairs={{0,4},{1,5},{2,6},{3,7},{4,0},{5,1},{6,2},{7,3},{8,12},{9,13},{10,... | collective-permute-start | bytes 983048 | tf_op jit(solution)/shard_map/ppermute | solution.py:26
  21.4 15.9 %collective-permute-start.7 = (bf16[80,2048]{1,0:T(8,128)(2,1)S(1)}, bf16[80,2048]{1,0:T(8,128)(2,1)S(1)}, u32[]{:S(2)}, u32[]{:S(2)}) collective-permute-start(bf16[80,2048]{1,0:T(8,128)(2,1)S(1)} %get-tuple-element.39), channel_id=1, source_target_pairs={{0,6},{1,7},{2,4},{3,5},{4,2},{5,3},{6,0},{7,1},{8,14},{9,15},{10,... | collective-permute-start | bytes 983048 | tf_op jit(solution)/shard_map/ppermute | solution.py:26
  31.3 12.3 %collective-permute-start.10 = (bf16[80,2432]{1,0:T(8,128)(2,1)S(1)}, bf16[80,2432]{1,0:T(8,128)(2,1)S(1)}, u32[]{:S(2)}, u32[]{:S(2)}) collective-permute-start(bf16[80,2432]{1,0:T(8,128)(2,1)S(1)} %get-tuple-element.46), channel_id=1, source_target_pairs={{0,1},{1,0},{2,3},{3,2},{4,5},{5,4},{6,7},{7,6},{8,9},{9,8},{10,11... | collective-permute-start | bytes 1167368 | tf_op jit(solution)/shard_map/ppermute | solution.py:26
  32.6 9.6 %collective-permute-start.11 = (bf16[40,2432]{1,0:T(8,128)(2,1)S(1)}, bf16[40,2432]{1,0:T(8,128)(2,1)S(1)}, u32[]{:S(2)}, u32[]{:S(2)}) collective-permute-start(bf16[40,2432]{1,0:T(8,128)(2,1)S(1)} %get-tuple-element.36.refs_8_), channel_id=1, source_target_pairs={{0,1},{1,0},{2,3},{3,2},{4,5},{5,4},{6,7},{7,6},{8,9},{9,8},{10,11... | collective-permute-start | bytes 583688 | tf_op jit(solution)/shard_map/ppermute | solution.py:26
  37.2 23.3 %collective-permute-start.6 = (bf16[80,2048]{1,0:T(8,128)(2,1)S(1)}, bf16[80,2048]{1,0:T(8,128)(2,1)S(1)}, u32[]{:S(2)}, u32[]{:S(2)}) collective-permute-start(bf16[80,2048]{1,0:T(8,128)(2,1)S(1)} %expert.4), channel_id=1, source_target_pairs={{0,4},{1,5},{2,6},{3,7},{4,0},{5,1},{6,2},{7,3},{8,12},{9,13},{10,... | collective-permute-start | bytes 983048 | tf_op jit(solution)/shard_map/ppermute | solution.py:26
  42.0 28.0 %copy-start = (s32[128,1]{0,1:T(1,128)S(1)}, s32[128,1]{0,1:T(1,128)}, u32[]{:S(2)}) copy-start(s32[128,1]{0,1:T(1,128)} %param.10) | copy-start | bytes 1540
  42.0 28.0 %copy-start.1 = (f32[128]{0:T(128)S(1)}, f32[128]{0:T(128)}, u32[]{:S(2)}) copy-start(f32[128]{0:T(128)} %param.9) | copy-start | bytes 1540
  42.1 1.5 %collective-permute-start.9 = (bf16[40,2432]{1,0:T(8,128)(2,1)S(1)}, bf16[40,2432]{1,0:T(8,128)(2,1)S(1)}, u32[]{:S(2)}, u32[]{:S(2)}) collective-permute-start(bf16[40,2432]{1,0:T(8,128)(2,1)S(1)} %get-tuple-element.45), channel_id=1, source_target_pairs={{0,1},{1,0},{2,3},{3,2},{4,5},{5,4},{6,7},{7,6},{8,9},{9,8},{10,11... | collective-permute-start | bytes 583688 | tf_op jit(solution)/shard_map/ppermute | solution.py:26
  45.5 26.0 %collective-permute-start.12 = (bf16[96,2048]{1,0:T(8,128)(2,1)S(1)}, bf16[96,2048]{1,0:T(8,128)(2,1)S(1)}, u32[]{:S(2)}, u32[]{:S(2)}) collective-permute-start(bf16[96,2048]{1,0:T(8,128)(2,1)S(1)} %get-tuple-element.48), channel_id=1, source_target_pairs={{0,8},{8,0},{16,24},{24,16},{1,9},{9,1},{17,25},{25,17},{2,10},{10... | collective-permute-start | bytes 1179656 | tf_op jit(solution)/shard_map/ppermute | solution.py:26
  47.1 24.4 %collective-permute-start.13 = (bf16[96,2048]{1,0:T(8,128)(2,1)S(1)}, bf16[96,2048]{1,0:T(8,128)(2,1)S(1)}, u32[]{:S(2)}, u32[]{:S(2)}) collective-permute-start(bf16[96,2048]{1,0:T(8,128)(2,1)S(1)} %get-tuple-element.49), channel_id=1, source_target_pairs={{0,16},{8,24},{16,0},{24,8},{1,17},{9,25},{17,1},{25,9},{2,18},{10... | collective-permute-start | bytes 1179656 | tf_op jit(solution)/shard_map/ppermute | solution.py:26
  48.7 22.8 %collective-permute-start.14 = (bf16[96,2048]{1,0:T(8,128)(2,1)S(1)}, bf16[96,2048]{1,0:T(8,128)(2,1)S(1)}, u32[]{:S(2)}, u32[]{:S(2)}) collective-permute-start(bf16[96,2048]{1,0:T(8,128)(2,1)S(1)} %get-tuple-element.50), channel_id=1, source_target_pairs={{0,24},{8,16},{16,8},{24,0},{1,25},{9,17},{17,9},{25,1},{2,26},{10... | collective-permute-start | bytes 1179656 | tf_op jit(solution)/shard_map/ppermute | solution.py:26
  49.1 11.4 %collective-permute-start.8 = (bf16[80,2048]{1,0:T(8,128)(2,1)S(1)}, bf16[80,2048]{1,0:T(8,128)(2,1)S(1)}, u32[]{:S(2)}, u32[]{:S(2)}) collective-permute-start(bf16[80,2048]{1,0:T(8,128)(2,1)S(1)} %get-tuple-element.40), channel_id=1, source_target_pairs={{0,6},{1,7},{2,4},{3,5},{4,2},{5,3},{6,0},{7,1},{8,14},{9,15},{10,... | collective-permute-start | bytes 983048 | tf_op jit(solution)/shard_map/ppermute | solution.py:26
  60.5 9.6 %collective-permute-start.4 = (bf16[80,2048]{1,0:T(8,128)(2,1)S(1)}, bf16[80,2048]{1,0:T(8,128)(2,1)S(1)}, u32[]{:S(2)}, u32[]{:S(2)}) collective-permute-start(bf16[80,2048]{1,0:T(8,128)(2,1)S(1)} %get-tuple-element.33), channel_id=1, source_target_pairs={{0,2},{1,3},{2,0},{3,1},{4,6},{5,7},{6,4},{7,5},{8,10},{9,11},{10,... | collective-permute-start | bytes 983048 | tf_op jit(solution)/shard_map/ppermute | solution.py:26
